TPU v7x, 32 devices: a whole 2x2x4 slice. The times are simulated.
32 devices in a mesh: ctx: 8 (over z, x), head: 4 (over y, core).
Axes of the slice: x: 2, y: 2, z: 4, core: 2. Of those that a mesh axis runs over, the one named last changes fastest.
Arguments:
- span_query: bfloat16 [2048, 16384], P('ctx', 'head'), may hold values from -5 to 5
- span_key: bfloat16 [2048, 1024], P('ctx', 'head'), may hold values from -12 to 12
- span_value: bfloat16 [2048, 1024], P('ctx', 'head'), may hold values from -6 to 6
- block_lists: int32 [16, 6], replicated, may hold values from 0 to 15, all different within a row
- owners: int32 [16], replicated, may hold values from 0 to 7, as said below
- cache_key: bfloat16 [32768, 1024], P('ctx', 'head'), may hold values from -12 to 12
- cache_value: bfloat16 [32768, 1024], P('ctx', 'head'), may hold values from -6 to 6
- sample_query: bfloat16 [64, 16384], P(None, 'head'), may hold values from -5 to 5
- sample_key: bfloat16 [64, 1024], P(None, 'head'), may hold values from -24 to 24
- sample_value: bfloat16 [64, 1024], P(None, 'head'), may hold values from -6 to 6
- out_weight: bfloat16 [16384, 16384], P('head', 'ctx'), may hold values from -0.046875 to 0.046875
Outputs:
- span_out: bfloat16 [2048, 16384], P('ctx', 'head')
- sample_out: bfloat16 [64, 16384], P(None, 'ctx')
- appended_key: bfloat16 [8192, 1024], P('ctx', 'head')
- appended_value: bfloat16 [8192, 1024], P('ctx', 'head')
Inputs may be any that keep to these rules, and one draw needn't show every extreme that they name: `block_lists`: each row lists 6 different key blocks. `owners`: no owner has more than 8 blocks, and some owner has exactly 8.
All inputs are finite; a program needn't handle non-finite values.
Results may differ from a plain program's by a relative error of at most 0.00245.
The roundings to bfloat16 on the way count: a program that leaves them out, or rounds other values in their place, can miss the bound.
Values may be sent and summed in bfloat16 or wider, within the bound.
A program may use at most 128 MiB of HBM per device.

v0:
```python
import jax
import jax.numpy as jnp
from jax import lax
from jax.sharding import PartitionSpec as P

HD = 128
BLOCK = 128
MOST_BLOCKS = 8


NEG = -1e30


def decode_partial(queries, keys, values, scale):
    scores = (
        jnp.einsum("skgd,bwkd->kgsbw", queries, keys, preferred_element_type=jnp.float32) * scale
    )
    peak = jnp.max(scores, axis=-1)
    weights = jnp.exp(scores - peak[..., None])
    total = jnp.sum(weights, axis=-1)
    summed = jnp.einsum(
        "kgsbw,bwkd->kgsbd",
        weights.astype(jnp.bfloat16),
        values,
        preferred_element_type=jnp.float32,
    )
    return (peak, total, summed)


def fold_groups(peak, total, summed):
    top = jnp.max(peak, axis=3)
    factor = jnp.exp(peak - top[..., None])
    return (top, jnp.sum(factor * total, axis=3), jnp.sum(factor[..., None] * summed, axis=3))


def finish_rows(top, total, combined, own_score, own_values):
    final_top = jnp.maximum(top, own_score)
    old_factor = jnp.exp(top - final_top)
    own_factor = jnp.exp(own_score - final_top)
    total = total * old_factor + own_factor
    combined = combined * old_factor[..., None] + own_factor[..., None] * own_values
    attended = (combined / total[..., None]).astype(jnp.bfloat16)
    samples = attended.shape[2]
    return jnp.transpose(attended, (2, 0, 1, 3)).reshape(samples, -1)


def local(
    span_query,
    span_key,
    span_value,
    block_lists,
    owners,
    cache_key,
    cache_value,
    sample_query,
    sample_key,
    sample_value,
    out_weight,
):
    scale = HD ** (-0.5)
    tokens = span_query.shape[0]
    kvh = span_key.shape[1] // HD
    group = span_query.shape[1] // HD // kvh
    qblk = tokens // BLOCK
    samples = sample_query.shape[0]
    position = lax.axis_index("ctx")
    gathered_key, gathered_value = (
        lax.all_gather(span_key, "ctx", axis=0, tiled=True),
        lax.all_gather(span_value, "ctx", axis=0, tiled=True),
    )
    key_blocks = gathered_key.reshape(-1, BLOCK, kvh, HD)
    value_blocks = gathered_value.reshape(-1, BLOCK, kvh, HD)
    block_count = key_blocks.shape[0]
    first = position * qblk
    listed = lax.dynamic_slice_in_dim(block_lists, first, qblk, 0)
    own = first + jnp.arange(qblk, dtype=jnp.int32)
    chosen = jnp.concatenate([own[:, None], listed], axis=1)
    width = chosen.shape[1] * BLOCK
    keys = jnp.take(key_blocks, chosen, axis=0).reshape(qblk, width, kvh, HD)
    values = jnp.take(value_blocks, chosen, axis=0).reshape(qblk, width, kvh, HD)
    queries = span_query.reshape(qblk, BLOCK, kvh, group, HD)
    scores = (
        jnp.einsum("bqkgd,bnkd->bkgqn", queries, keys, preferred_element_type=jnp.float32) * scale
    )
    column = jnp.arange(width, dtype=jnp.int32)
    which = column // BLOCK
    within = column % BLOCK
    row_ids = jnp.arange(BLOCK, dtype=jnp.int32)
    causal = within[None, :] <= row_ids[:, None]
    elsewhere = chosen[:, which] != own[:, None]
    allowed = jnp.where((which == 0)[None, None, :], causal[None, :, :], elsewhere[:, None, :])
    scores = jnp.where(allowed[:, None, None, :, :], scores, NEG)
    peak = jnp.max(scores, axis=-1, keepdims=True)
    weights = jnp.exp(scores - peak)
    probs = (weights / jnp.sum(weights, axis=-1, keepdims=True)).astype(jnp.bfloat16)
    prefill = jnp.einsum("bkgqn,bnkd->bqkgd", probs, values, preferred_element_type=jnp.float32)
    span_out = prefill.astype(jnp.bfloat16).reshape(tokens, kvh * group * HD)
    mine = (owners == position).astype(jnp.int32)
    rank = jnp.cumsum(mine) - 1
    slot_ids = jnp.arange(MOST_BLOCKS, dtype=jnp.int32)
    hits = (mine[None, :] == 1) & (rank[None, :] == slot_ids[:, None])
    picked = jnp.sum(jnp.where(hits, jnp.arange(block_count, dtype=jnp.int32)[None, :], 0), axis=1)
    live = jnp.any(hits, axis=1)
    slot_keys = jnp.where(
        live[:, None, None, None], key_blocks[picked], jnp.zeros((), jnp.bfloat16)
    )
    slot_values = jnp.where(
        live[:, None, None, None], value_blocks[picked], jnp.zeros((), jnp.bfloat16)
    )
    appended_key = slot_keys.reshape(MOST_BLOCKS * BLOCK, kvh * HD)
    appended_value = slot_values.reshape(MOST_BLOCKS * BLOCK, kvh * HD)
    asked = sample_query.reshape(samples, kvh, group, HD)
    res_peak, res_total, res_sum = decode_partial(
        asked, cache_key.reshape(1, -1, kvh, HD), cache_value.reshape(1, -1, kvh, HD), scale
    )
    blk_peak, blk_total, blk_sum = decode_partial(asked, slot_keys, slot_values, scale)
    blk_peak = jnp.where(live, blk_peak, NEG)
    blk_total = jnp.where(live, blk_total, 0.0)
    blk_sum = jnp.where(live[:, None], blk_sum, 0.0)
    peak_local, total_local, sum_local = fold_groups(
        jnp.concatenate([res_peak, blk_peak], axis=3),
        jnp.concatenate([res_total, blk_total], axis=3),
        jnp.concatenate([res_sum, blk_sum], axis=3),
    )
    own_keys = sample_key.reshape(samples, kvh, HD)
    own_score = (
        jnp.einsum("skgd,skd->kgs", asked, own_keys, preferred_element_type=jnp.float32) * scale
    )
    own_values = jnp.transpose(
        sample_value.reshape(samples, kvh, HD).astype(jnp.float32), (1, 0, 2)
    )[:, None, :, :]
    top = lax.pmax(peak_local, "ctx")
    factor = jnp.exp(peak_local - top)
    total, combined = lax.psum((total_local * factor, sum_local * factor[..., None]), "ctx")
    attended = finish_rows(top, total, combined, own_score, own_values)
    partial_out = jnp.dot(attended, out_weight, preferred_element_type=jnp.float32)
    sample_out = lax.psum(partial_out, "head").astype(jnp.bfloat16)
    return (span_out, sample_out, appended_key, appended_value)


def solution(mesh):
    return jax.shard_map(
        local,
        mesh=mesh,
        in_specs=(
            P("ctx", "head"),
            P("ctx", "head"),
            P("ctx", "head"),
            P(),
            P(),
            P("ctx", "head"),
            P("ctx", "head"),
            P(None, "head"),
            P(None, "head"),
            P(None, "head"),
            P("head", "ctx"),
        ),
        out_specs=(P("ctx", "head"), P(None, "ctx"), P("ctx", "head"), P("ctx", "head")),
        check_vma=False,
    )
```

profile of v0, /device:TPU:0, one launch (start us, length us, event | category | flops | bytes accessed | tf_op | source)
XLA Modules:
  0.0 272.5 jit_solution(17090528093236956477)
XLA Ops:
  7.2 0.7 all-gather.5.cloned.1.call-update
  8.0 0.7 all-gather.3.cloned.1.call-update
  8.8 0.1 constant_dynamic-slice_fusion
  8.8 0.1 copy.243
  8.9 0.1 compare_and_fusion
  9.0 0.1 copy.191
  9.1 0.7 fusion.63
  9.8 0.1 copy.202
  9.9 0.1 add_reduce_fusion
  10.1 0.1 fusion.59
  10.2 0.1 select_reduce_fusion
  10.3 0.1 reshape.312
  10.4 0.1 broadcast_bitcast_fusion
  10.5 0.8 reshape.328
  11.3 0.8 bitcast_bitcast_fusion
  12.0 0.2 iota_compare_fusion
  12.2 1.9 gather_fusion
  14.2 0.2 copy.192
  14.4 1.2 copy.246
  15.6 0.4 fusion.39
  15.9 0.1 copy.226
  16.0 3.4 %copy.245 = bf16[32,8,32,128]{3,2,1,0:T(8,128)(2,1)} copy(bf16[32,8,32,128]{3,1,2,0:T(8,128)(2,1)} %bitcast.150) | data formatting | bytes 4194304
  19.4 2.6 reshape.260
  22.0 4.0 %reshape.264 = bf16[4096,2,128]{2,1,0:T(2,128)(2,1)} reshape(bf16[4096,256]{1,0:T(8,128)(2,1)} %param.19) | data formatting | bytes 4194304 | tf_op jit(solution)/shard_map/reshape.6
  26.0 13.2 %bitcast_reduce_fusion = (f32[2,16,64]{2,1,0:T(8,128)S(1)}, f32[2,4096,64,16]{1,2,3,0:T(8,128)}) fusion(bf16[64,2,16,128]{3,2,1,0:T(8,128)(2,1)S(1)} %bitcast.145, bf16[4096,2,128,1]{2,1,0,3:T(2,128)(2,1)S(1)} %bitcast.143), kind=kOutput, calls=%fused_computation.7 | convolution fusion | flops 2164258816 | bytes 36184064 | tf_op jit(solution)/shard_map/skgd,bwkd->kgsbw/dot_general | solution.py:16
  39.2 0.8 broadcast_select_fusion.3
  40.0 14.5 %fusion.28 = f32[2,16,64,1,128]{4,2,1,3,0:T(8,128)} fusion(bf16[4096,2,128,1]{2,1,0,3:T(2,128)(2,1)S(1)} %bitcast.152, f32[2,4096,64,16]{1,2,3,0:T(8,128)} %get-tuple-element.52, f32[2,16,64]{2,1,0:T(8,128)S(1)} %get-tuple-element.51), kind=kOutput, calls=%fused_computation.37 | convolution fusion | flops 2172649472 | bytes 36708352 | tf_op jit(solution)/shard_map/kgsbw,bwkd->kgsbd/dot_general | solution.py:21
  54.5 14.1 %fusion.2 = f32[2,16,64]{2,1,0:T(8,128)S(1)} fusion(f32[2,4096,64,16]{1,2,3,0:T(8,128)} %get-tuple-element.52, f32[2,16,64]{2,1,0:T(8,128)S(1)} %get-tuple-element.51), kind=kLoop, calls=%fused_computation.12 | loop fusion | flops 25163776 | bytes 33570816 | tf_op jit(solution)/shard_map/reduce_sum | solution.py:20
  68.5 1.4 reshape.331
  69.9 0.2 copy.194
  70.2 24.1 %all-gather.3.cloned.1.call-done = bf16[2048,256]{1,0:T(8,128)(2,1)} async-done(((bf16[256,256]{1,0:T(8,128)(2,1)}), bf16[2048,256]{1,0:T(8,128)(2,1)}) %all-gather.3.cloned.1.call-update) | async-done | bytes 1048592 | tf_op jit(solution)/shard_map/all_gather | solution.py:69
  94.3 2.2 reshape.330
  96.5 1.5 copy.189
  97.9 0.7 gather_fusion.2
  98.6 1.6 gather_fusion.3
  100.2 0.6 gather_fusion.1
  100.9 1.6 gather_fusion.4
  102.5 1.7 broadcast_select_fusion
  104.2 1.0 copy.195
  105.2 1.0 copy.190
  106.2 0.1 broadcast_select_fusion.2
  106.3 2.5 bitcast_reduce_fusion.1
  108.8 4.7 %fusion.15 = (bf16[2,16,64,8,128]{4,2,1,3,0:T(8,128)(2,1)S(1)}, f32[2,16,64,8]{2,1,3,0:T(8,128)S(1)}) fusion(f32[2,8,128,64,16]{2,3,4,1,0:T(8,128)S(1)} %get-tuple-element.50, f32[2,16,64,8]{2,1,3,0:T(8,128)S(1)} %get-tuple-element.49), kind=kLoop, calls=%fused_computation.28 | loop fusion | flops 8372224 | bytes 12713984 | tf_op jit(solution)/shard_map/convert_element_type | solution.py:23
  113.6 0.1 fusion.71
  113.7 1.2 fusion.41
  114.9 4.3 %select_bitcast_fusion = f32[2,16,64,8,128]{4,2,1,3,0:T(8,128)} fusion(f32[2,8,128,16,64]{2,4,3,1,0:T(8,128)S(1)} %bitcast.141, pred[8]{0:T(512)(128)(4,1)S(1)} %fusion.59), kind=kLoop, calls=%fused_computation.26 | loop fusion | flops 2097152 | bytes 16777224 | tf_op jit(solution)/shard_map/jit(_where)/select_n | solution.py:119
  119.2 34.9 %pmax.7 = f32[2,16,64]{2,1,0:T(8,128)S(1)} all-reduce(f32[2,16,64]{2,1,0:T(8,128)S(1)} %reduce_max.47), channel_id=1, replica_groups=mesh['ctx'=8,'head'=4] {'ctx'}, use_global_device_ids=true, to_apply=%region_9.11 | all-reduce | flops 2048 | bytes 16384 | tf_op jit(solution)/shard_map/pmax | solution.py:132
  154.2 6.4 %fusion.12 = f32[2,16,64,128]{3,2,1,0:T(8,128)S(1)} fusion(f32[2,16,64,8,128]{4,2,1,3,0:T(8,128)} %select_bitcast_fusion, f32[2,16,64,1,128]{4,2,1,3,0:T(8,128)S(1)} %copy-done.3, f32[2,16,64,9]{2,1,3,0:T(8,128)S(1)} %get-tuple-element.31), kind=kLoop, calls=%fused_computation.22 | loop fusion | flops 6815744 | bytes 10559488 | tf_op jit(solution)/shard_map/reduce_sum | solution.py:33
  160.6 1.3 broadcast_multiply_fusion
  161.9 16.4 %fusion.72 = (f32[2,2,16,128]{3,2,1,0:T(8,128)S(1)}, f32[2,2,16,128,896]{3,4,2,1,0:T(8,128)}) fusion(pred[2,128,896]{1,2,0:T(8,128)(4,1)S(1)} %broadcast_select_fusion.3, bf16[2,896,2,128,1]{3,1,4,2,0:T(8,128)(2,1)} %bitcast.155, bf16[2,128,2,16,128]{4,3,2,1,0:T(8,128)(2,1)} %bitcast.151), kind=kOutput, calls=%fused_computation.120 | convolution fusion | flops 1908409216 | bytes 32636928 | tf_op jit(solution)/shard_map/sub | solution.py:94
  178.3 13.7 %convert_bitcast_fusion = bf16[2,128,2,16,128]{1,4,3,2,0:T(8,128)(2,1)} fusion(bf16[2,896,2,128,1]{3,1,4,2,0:T(8,128)(2,1)S(1)} %bitcast.156, f32[2,2,16,128,896]{3,4,2,1,0:T(8,128)} %get-tuple-element.48, f32[2,2,16,128]{3,2,1,0:T(8,128)S(1)} %get-tuple-element.47), kind=kOutput, calls=%fused_computation.33 | convolution fusion | flops 1894776832 | bytes 32407552 | tf_op jit(solution)/shard_map/bkgqn,bnkd->bqkgd/dot_general | solution.py:96
  191.9 0.3 copy.213
  192.3 0.3 copy.214
  192.6 0.1 bitcast_select_fusion.4
  192.7 1.0 copy.216
  193.7 1.0 copy.215
  194.7 3.4 %copy.199 = bf16[2,128,2,16,128]{4,3,2,1,0:T(8,128)(2,1)S(1)} copy(bf16[2,128,2,16,128]{1,4,3,2,0:T(8,128)(2,1)} %convert_bitcast_fusion) | data formatting | bytes 4194304 | tf_op jit(solution)/shard_map/convert_element_type | solution.py:97
  198.2 2.3 reshape.259
  200.5 33.6 %psum.22 = f32[2,16,64]{2,1,0:T(8,128)S(1)} all-reduce(f32[2,16,64]{2,1,0:T(8,128)S(1)} %get-tuple-element.28), channel_id=1, replica_groups=mesh['ctx'=8,'head'=4] {'ctx'}, use_global_device_ids=true, to_apply=%region_14.16 | all-reduce | flops 2048 | bytes 16384 | tf_op jit(solution)/shard_map/psum | solution.py:134
  234.1 3.5 %all-reduce.3.cloned.1.call-done = f32[2,16,64,128]{3,2,1,0:T(8,128)} async-done(((f32[2,16,64,128]{3,2,1,0:T(8,128)}), f32[2,16,64,128]{3,2,1,0:T(8,128)}) %all-reduce.3.cloned.1.call-update) | async-done | bytes 1048592 | tf_op jit(solution)/shard_map/psum | solution.py:134
  237.6 2.0 fusion.44
  239.7 0.3 copy.212
  240.0 8.8 %fusion.33 = f32[64,2048]{1,0:T(8,128)S(1)} fusion(bf16[4096,2048]{1,0:T(8,128)(2,1)} %param.23, bf16[8,8,32,128]{3,2,1,0:T(8,128)(2,1)S(1)} %bitcast.149), kind=kOutput, calls=%fused_computation.43 | convolution fusion | flops 1073741824 | bytes 17825792 | tf_op jit(solution)/shard_map/dot_general | solution.py:136
  248.9 17.1 %all-reduce.4 = bf16[64,2048]{1,0:T(8,128)(2,1)} all-reduce(f32[64,2048]{1,0:T(8,128)S(1)} %fusion.33), channel_id=1, replica_groups=mesh['ctx'=8,'head'=4] {'head'}, use_global_device_ids=true, to_apply=%region_15.17 | all-reduce | flops 131072 | bytes 786432 | tf_op jit(solution)/shard_map/psum | solution.py:137
  (31 shorter events, 0.4 us)
Async XLA Ops:
  7.2 1.6 copy-start
  7.2 61.4 %all-gather.5.cloned.1.call-start = ((), (), s32[]{:S(2)}) async-start(), calls=%async_computation.1 | async-start | bytes 1179648 | tf_op jit(solution)/shard_map/all_gather | solution.py:68
  7.9 86.4 %all-gather.3.cloned.1.call-start = ((), (), s32[]{:S(2)}) async-start(), calls=%async_computation | async-start | bytes 1179648 | tf_op jit(solution)/shard_map/all_gather | solution.py:69
  8.7 229.0 %all-reduce.3.cloned.1.call-start = ((), (), s32[]{:S(2)}) async-start(), calls=%async_computation.2 | async-start | bytes 2097152 | tf_op jit(solution)/shard_map/psum | solution.py:134
  26.0 14.0 %copy-start.2 = (bf16[4096,2,128]{2,1,0:T(2,128)(2,1)S(1)}, bf16[4096,2,128]{2,1,0:T(2,128)(2,1)}, u32[]{:S(2)}) copy-start(bf16[4096,2,128]{2,1,0:T(2,128)(2,1)} %reshape.264) | copy-start | bytes 6291460
  114.9 39.3 %copy-start.3 = (f32[2,16,64,1,128]{4,2,1,3,0:T(8,128)S(1)}, f32[2,16,64,1,128]{4,2,1,3,0:T(8,128)}, u32[]{:S(2)}) copy-start(f32[2,16,64,1,128]{4,2,1,3,0:T(8,128)} %fusion.28) | copy-start | bytes 3145732
  161.9 16.4 %copy-start.4 = (bf16[2,7,128,2,128]{4,2,1,3,0:T(8,128)(2,1)S(1)}, bf16[2,7,128,2,128]{4,2,1,3,0:T(8,128)(2,1)}, u32[]{:S(2)}) copy-start(bf16[2,7,128,2,128]{4,2,1,3,0:T(8,128)(2,1)} %copy.190) | copy-start | bytes 2752516
  240.0 25.9 %copy-start.1 = (s32[16,6]{0,1:T(8,128)S(1)}, s32[16,6]{0,1:T(8,128)}, u32[]{:S(2)}) copy-start(s32[16,6]{0,1:T(8,128)} %param.16) | copy-start | bytes 1156
Sparse Core Ops, SparseCore 0:
  10.1 42.9 all-gather.4
  55.3 38.9 all-gather.2
  162.0 75.5 all-reduce.2
where the time goes:
time: 273 us; the launch traced here: 272 us
  blocking collectives  85.6 us (31%)
  matrix products  70.7 us (26%)
  other arithmetic  38 us (14%)
  local copies, waits for them, and re-layouts  35.1 us (13%)
  waiting for transfers between devices  29 us (11%)
  between operations  14.1 us (5%)
    pmax x1, blocking collectives, local(): top = lax.pmax(peak_local, 'ctx')  34.9 us
    psum x1, blocking collectives, local(): lax.psum((total_local * factor, sum_local * factor[..., None]), 'ctx')  33.6 us
    all_gather x1, waiting for transfers between devices, local(): lax.all_gather(span_value, 'ctx', axis=0, tiled=True)  24.1 us
    psum x1, blocking collectives, local(): sample_out = lax.psum(partial_out, 'head').astype(jnp.bfloat16)  17.1 us
    sub x1, matrix products, local(): weights = jnp.exp(scores - peak)  16.4 us
    dot_general x2, matrix products, decode_partial(): jnp.einsum('skgd,bwkd->kgsbw', queries, keys, preferred_element_type=jnp....  15.7 us
    dot_general x1, matrix products, decode_partial(): jnp.einsum('kgsbw,bwkd->kgsbd', weights.astype(jnp.bfloat16), values, pre...  14.5 us
    reduce_sum x1, other arithmetic, decode_partial(): total = jnp.sum(weights, axis=-1)  14.1 us
  transfers between devices with their start and end apart: 3, of which 2 were waited for; matrix products, arithmetic and copies ran while one was open for 37% of the time, Pallas kernels for 0%

commit v1 on v0

v1 whole, which is shorter than its diff:
```python
import functools

import jax
import jax.numpy as jnp
from jax import lax
from jax.experimental import pallas as pl
from jax.experimental.pallas import tpu as pltpu
from jax.sharding import PartitionSpec as P

HD = 128
BLOCK = 128
MOST_BLOCKS = 8
NEG = -1e30
SCALE = HD ** -0.5
EXP2_SCALE = SCALE * 1.4426950408889634


def dot_t(a, b):
    return lax.dot_general(a, b, (((1,), (1,)), ((), ())), preferred_element_type=jnp.float32)


def dot(a, b):
    return jnp.dot(a, b, preferred_element_type=jnp.float32)


def lane_fold(op, x):
    parts = [x[:, i * 128 : (i + 1) * 128] for i in range(x.shape[1] // 128)]
    while len(parts) > 1:
        parts = [op(*parts[i : i + 2]) if i + 1 < len(parts) else parts[i] for i in range(0, len(parts), 2)]
    return parts[0]


def column(ref, head, start, size):
    return ref[pl.ds(start, size), pl.ds(pl.multiple_of(head * HD, HD), HD)]


def decode_tile(dims, tile, q_ref, ck_ref, cv_ref, sk_ref, sv_ref, s_ref):
    samples, group, per, chunk = dims
    rows = per * samples
    head = (tile * per) // group
    q = jnp.concatenate([column(q_ref, tile * per + g, 0, samples) for g in range(per)], axis=0)
    resident = ck_ref.shape[0]
    high = jnp.full((rows, 128), NEG, jnp.float32)
    for c in range(resident // chunk):
        s = dot_t(q, column(ck_ref, head, c * chunk, chunk))
        s_ref[:, c * chunk : (c + 1) * chunk] = s
        high = jnp.maximum(high, lane_fold(jnp.maximum, s))
    peak = jnp.max(high, axis=1, keepdims=True)
    total = jnp.zeros((rows, 128), jnp.float32)
    acc = jnp.zeros((rows, HD), jnp.float32)
    for c in range(resident // chunk):
        w = jnp.exp2((s_ref[:, c * chunk : (c + 1) * chunk] - peak) * EXP2_SCALE)
        total = total + lane_fold(jnp.add, w)
        acc = acc + dot(w.astype(jnp.bfloat16), column(cv_ref, head, c * chunk, chunk))
    groups = [(peak, jnp.sum(total, axis=1, keepdims=True), acc)]
    for b in range(sk_ref.shape[0] // BLOCK):
        s = dot_t(q, column(sk_ref, head, b * BLOCK, BLOCK))
        top = jnp.max(s, axis=1, keepdims=True)
        w = jnp.exp2((s - top) * EXP2_SCALE)
        part = dot(w.astype(jnp.bfloat16), column(sv_ref, head, b * BLOCK, BLOCK))
        groups.append((top, jnp.sum(w, axis=1, keepdims=True), part))
    top = functools.reduce(jnp.maximum, [g[0] for g in groups])
    factors = [jnp.exp2((g[0] - top) * EXP2_SCALE) for g in groups]
    total = sum(f * g[1] for f, g in zip(factors, groups))
    acc = sum(f * g[2] for f, g in zip(factors, groups))
    return top, total, acc


def prefill_heads(heads, block, first_head, q_ref, keys, values, flags, causal, out_ref):
    for g in range(heads):
        q = column(q_ref, first_head + g, block * BLOCK, BLOCK)
        s = dot_t(q, keys)
        parts = [s[:, :BLOCK] + causal]
        for i, flag in enumerate(flags):
            parts.append(s[:, (i + 1) * BLOCK : (i + 2) * BLOCK] + flag)
        s = jnp.concatenate(parts, axis=1)
        peak = jnp.max(lane_fold(jnp.maximum, s), axis=1, keepdims=True)
        w = jnp.exp2((s - peak) * EXP2_SCALE)
        inverse = 1.0 / jnp.sum(lane_fold(jnp.add, w), axis=1, keepdims=True)
        probs = (w * inverse).astype(jnp.bfloat16)
        out_ref[pl.ds(block * BLOCK, BLOCK), pl.ds(pl.multiple_of((first_head + g) * HD, HD), HD)] = dot(
            probs, values
        ).astype(jnp.bfloat16)


def prefill_all(dims, position, lists_ref, q_ref, kg_ref, vg_ref, kc_ref, vc_ref, out_ref, between=None):
    qblk, kvh, group, ksel, heads = dims
    causal = jnp.where(
        lax.broadcasted_iota(jnp.int32, (BLOCK, BLOCK), 1) <= lax.broadcasted_iota(jnp.int32, (BLOCK, BLOCK), 0),
        0.0,
        NEG,
    ).astype(jnp.float32)
    for b in range(qblk):
        own = position * qblk + b
        kc_ref[:BLOCK, :] = kg_ref[own]
        vc_ref[:BLOCK, :] = vg_ref[own]
        flags = []
        for i in range(ksel):
            listed = lists_ref[own, i]
            kc_ref[(i + 1) * BLOCK : (i + 2) * BLOCK, :] = kg_ref[listed]
            vc_ref[(i + 1) * BLOCK : (i + 2) * BLOCK, :] = vg_ref[listed]
            flags.append(jnp.where(listed == own, NEG, 0.0).astype(jnp.float32))
        for k in range(kvh):

            def step(i, carry, b=b, k=k, flags=flags):
                prefill_heads(
                    heads,
                    b,
                    k * group + i * heads,
                    q_ref,
                    kc_ref[:, k * HD : (k + 1) * HD],
                    vc_ref[:, k * HD : (k + 1) * HD],
                    flags,
                    causal,
                    out_ref,
                )
                return carry

            lax.fori_loop(0, group // heads, step, 0)
            if between is not None:
                between(b * kvh + k)


def append_all(position, owners_ref, kg_ref, vg_ref, ak_ref, av_ref):
    blocks = kg_ref.shape[0]

    def count(b, carry):
        rank, picked = carry
        mine = owners_ref[b] == position
        picked = tuple(jnp.where(mine & (rank == slot), b, p) for slot, p in enumerate(picked))
        return rank + mine.astype(jnp.int32), picked

    rank, picked = lax.fori_loop(
        0, blocks, count, (jnp.int32(0), tuple(jnp.int32(0) for _ in range(MOST_BLOCKS)))
    )
    for slot in range(MOST_BLOCKS):
        live = jnp.broadcast_to(rank, (BLOCK, kg_ref.shape[2])) > slot
        rows = slice(slot * BLOCK, (slot + 1) * BLOCK)
        for src, dst in ((kg_ref, ak_ref), (vg_ref, av_ref)):
            x = src[picked[slot]].astype(jnp.float32)
            dst[rows, :] = jnp.where(live, x, 0.0).astype(jnp.bfloat16)


def decode_kernel(dims, tiles, q_ref, ck_ref, cv_ref, sk_ref, sv_ref, m_ref, l_ref, acc_ref, s_ref):
    samples, _, per, _ = dims

    def step(tile, carry):
        m, l, acc = decode_tile(dims, tile, q_ref, ck_ref, cv_ref, sk_ref, sv_ref, s_ref)
        m_ref[tile] = jnp.broadcast_to(m, acc.shape)
        l_ref[tile] = jnp.broadcast_to(l, acc.shape)
        acc_ref[tile] = acc
        return carry

    lax.fori_loop(0, tiles, step, 0)


def prefill_kernel(dims, lists_ref, owners_ref, q_ref, kg_ref, vg_ref, out_ref, ak_ref, av_ref, kc_ref, vc_ref):
    position = lax.axis_index("ctx")
    append_all(position, owners_ref, kg_ref, vg_ref, ak_ref, av_ref)
    prefill_all(dims, position, lists_ref, q_ref, kg_ref, vg_ref, kc_ref, vc_ref, out_ref)


VM = pl.BlockSpec(memory_space=pltpu.VMEM)
SM = pl.BlockSpec(memory_space=pltpu.SMEM)


def local(n_ctx, span_query, span_key, span_value, block_lists, owners, cache_key, cache_value, sample_query, sample_key, sample_value, out_weight):
    tokens = span_query.shape[0]
    kvh = span_key.shape[1] // HD
    group = span_query.shape[1] // HD // kvh
    qblk = tokens // BLOCK
    samples = sample_query.shape[0]
    per = kvh * group // n_ctx
    resident = cache_key.shape[0]
    kg = lax.all_gather(span_key, "ctx", axis=0, tiled=True).reshape(-1, BLOCK, kvh * HD)
    vg = lax.all_gather(span_value, "ctx", axis=0, tiled=True).reshape(-1, BLOCK, kvh * HD)
    dims = (samples, group, per, 512)
    f32 = jax.ShapeDtypeStruct((n_ctx, per * samples, HD), jnp.float32)
    m, l, acc = pl.pallas_call(
        functools.partial(decode_kernel, dims, n_ctx),
        out_shape=(f32, f32, f32),
        in_specs=[VM] * 5,
        out_specs=(VM,) * 3,
        scratch_shapes=[pltpu.VMEM((per * samples, resident), jnp.float32)],
        compiler_params=pltpu.CompilerParams(vmem_limit_bytes=60 << 20),
        cost_estimate=pl.CostEstimate(flops=5 << 30, bytes_accessed=8 << 20, transcendentals=9 << 20),
        name="decode",
    )(sample_query, cache_key, cache_value, span_key, span_value)
    width = (block_lists.shape[1] + 1) * BLOCK
    slots = jax.ShapeDtypeStruct((MOST_BLOCKS * BLOCK, kvh * HD), jnp.bfloat16)
    span_out, appended_key, appended_value = pl.pallas_call(
        functools.partial(prefill_kernel, (qblk, kvh, group, block_lists.shape[1], 4)),
        out_shape=(jax.ShapeDtypeStruct(span_query.shape, jnp.bfloat16), slots, slots),
        in_specs=[SM, SM, VM, VM, VM],
        out_specs=(VM,) * 3,
        scratch_shapes=[pltpu.VMEM((width, kvh * HD), jnp.bfloat16)] * 2,
        compiler_params=pltpu.CompilerParams(vmem_limit_bytes=60 << 20),
        cost_estimate=pl.CostEstimate(flops=4 << 30, bytes_accessed=8 << 20, transcendentals=7 << 20),
        name="prefill",
    )(block_lists, owners, span_query, kg, vg)
    m, l = m[:, :, :1] * SCALE, l[:, :, :1]
    top = lax.pmax(m, "ctx")
    factor = jnp.exp(m - top)
    l, acc = lax.psum((l * factor, acc * factor), "ctx")
    shape = (kvh, group, samples, -1)
    top, l, acc = top.reshape(shape), l.reshape(shape), acc.reshape(shape)
    asked = sample_query.reshape(samples, kvh, group, HD)
    own_keys = sample_key.reshape(samples, kvh, HD)
    own = jnp.einsum("skgd,skd->kgs", asked, own_keys, preferred_element_type=jnp.float32)[..., None] * SCALE
    own_values = jnp.transpose(sample_value.reshape(samples, kvh, HD).astype(jnp.float32), (1, 0, 2))[:, None]
    final = jnp.maximum(top, own)
    old, new = jnp.exp(top - final), jnp.exp(own - final)
    attended = ((acc * old + new * own_values) / (l * old + new)).astype(jnp.bfloat16)
    attended = jnp.transpose(attended, (2, 0, 1, 3)).reshape(samples, -1)
    partial_out = jnp.dot(attended, out_weight, preferred_element_type=jnp.float32)
    sample_out = lax.psum(partial_out, "head").astype(jnp.bfloat16)
    return span_out, sample_out, appended_key, appended_value


def solution(mesh):
    c = P("ctx", "head")
    return jax.shard_map(
        functools.partial(local, mesh.shape["ctx"]),
        mesh=mesh,
        in_specs=(c, c, c, P(), P(), c, c, P(None, "head"), P(None, "head"), P(None, "head"), P("head", "ctx")),
        out_specs=(c, P(None, "ctx"), c, c),
        check_vma=False,
    )
```

time: 273 us -> 308 us (1.13)
  waiting for transfers between devices: 29 us -> 94.6 us
  matrix products: 70.7 us -> 9.19 us
  Pallas kernels: 0 us -> 53 us
  blocking collectives: 85.6 us -> 127 us
  local copies, waits for them, and re-layouts: 35.1 us -> 2.91 us
  other arithmetic: 38 us -> 7.35 us
    pallas_call x0 -> x2, Pallas kernels: none -> 53 us  [the longest x1 34.6 us: local(): pl.pallas_call(functools.partial(prefill_kernel, (qblk, kvh, group, block...]
    dot_general x4 -> x0, matrix products: 43.8 us -> none  [the longest x2 15.7 us: decode_partial(): jnp.einsum('skgd,bwkd->kgsbw', queries, keys, preferred_element_type=jnp....]
    pmax x1, blocking collectives: 34.9 us -> 73.8 us  [local(): top = lax.pmax(m, 'ctx')]
    psum x1, waiting for transfers between devices: 3.49 us -> 38.6 us  [local(): l, acc = lax.psum((l * factor, acc * factor), 'ctx')]
    reduce_sum x4 -> x0, other arithmetic: 20.6 us -> none  [the longest x1 14.1 us: decode_partial(): total = jnp.sum(weights, axis=-1)]
    all_gather x1, waiting for transfers between devices: 24.1 us -> 41.2 us  [local(): lax.all_gather(span_value, 'ctx', axis=0, tiled=True)]
    sub x1 -> x0, matrix products: 16.4 us -> none  [local(): weights = jnp.exp(scores - peak)]
    all_gather x1, waiting for transfers between devices: 0.01 us -> 13.4 us  [local(): lax.all_gather(span_key, 'ctx', axis=0, tiled=True)]
  transfers between devices with their start and end apart: 3 -> 3, of which waited for: 2 -> 3; matrix products, arithmetic and copies ran while one was open for 37% -> 4% of each run, Pallas kernels for 0% -> 0%
where the time goes in v1:
time: 308 us
  blocking collectives  127 us (41%)
  waiting for transfers between devices  94.6 us (31%)
  Pallas kernels  53 us (17%)
  between operations  13.9 us (5%)
  matrix products  9.19 us (3%)
  other arithmetic  7.35 us (2%)
    pmax x1, blocking collectives, local(): top = lax.pmax(m, 'ctx')  73.8 us
    all_gather x1, waiting for transfers between devices, local(): lax.all_gather(span_value, 'ctx', axis=0, tiled=True)  41.2 us
    psum x1, waiting for transfers between devices, local(): l, acc = lax.psum((l * factor, acc * factor), 'ctx')  38.6 us
    psum x1, blocking collectives, local(): l, acc = lax.psum((l * factor, acc * factor), 'ctx')  35.5 us
    pallas_call x1, Pallas kernels, local(): pl.pallas_call(functools.partial(prefill_kernel, (qblk, kvh, group, block...  34.6 us
    pallas_call x1, Pallas kernels, local(): pl.pallas_call(functools.partial(decode_kernel, dims, n_ctx), out_shape=(...  18.4 us
    psum x1, blocking collectives, local(): sample_out = lax.psum(partial_out, 'head').astype(jnp.bfloat16)  17.8 us
    all_gather x1, waiting for transfers between devices, local(): lax.all_gather(span_key, 'ctx', axis=0, tiled=True)  13.4 us
  transfers between devices with their start and end apart: 3, of which 3 were waited for; matrix products, arithmetic and copies ran while one was open for 4% of the time, Pallas kernels for 0%

profile of v1, /device:TPU:0, one launch (start us, length us, event | category | flops | bytes accessed | tf_op | source)
XLA Modules:
  0.0 308.1 jit_solution(13874325314365499545)
XLA Ops:
  7.2 0.0 copy-start
  7.2 0.0 copy-start.2
  7.2 0.0 copy-start.1
  7.2 0.0 copy-start.3
  7.2 0.0 all-reduce.3.cloned.1.call-start
  7.3 18.4 %decode.1 = (f32[8,256,128]{2,1,0:T(8,128)}, f32[8,256,128]{2,1,0:T(8,128)}, f32[8,256,128]{2,1,0:T(8,128)}) custom-call(bf16[64,4096]{1,0:T(8,128)(2,1)} %q_ref.3, bf16[4096,256]{1,0:T(8,128)(2,1)} %ck_ref.1, bf16[4096,256]{1,0:T(8,128)(2,1)} %cv_ref.1, bf16[256,256]{1,0:T(8,128)(2,1)} %sk_ref.1, bf16[256,256]{1,0:T(8,128)(2,1)} %sv_ref.1), custom_call_target="tpu_custom_call" | custom-call | flops 5368709120 | bytes 8388608 | tf_op jit(solution)/shard_map/decode/pallas_call | solution.py:179
  25.7 1.3 slice_multiply_fusion
  27.0 73.8 %pmax.7 = f32[8,256,1]{2,1,0:T(8,128)S(1)} all-reduce(f32[8,256,1]{2,1,0:T(8,128)S(1)} %slice_multiply_fusion), channel_id=1, replica_groups=mesh['ctx'=8,'head'=4] {'ctx'}, use_global_device_ids=true, to_apply=%region_0.0 | all-reduce | flops 2048 | bytes 16384 | tf_op jit(solution)/shard_map/pmax | solution.py:202
  100.8 2.4 multiply_reduce_fusion
  103.3 1.6 broadcast_multiply_fusion
  104.8 1.6 copy.18
  106.4 0.0 all-reduce.3.cloned.1.call-update
  106.4 0.0 all-gather.3.cloned.1.call-start
  106.5 0.7 all-gather.3.cloned.1.call-update
  107.2 0.0 all-gather.5.cloned.1.call-start
  107.2 0.7 all-gather.5.cloned.1.call-update
  107.9 0.1 reshape.56
  108.0 35.5 %psum.22 = f32[2,16,64]{2,1,0:T(8,128)S(1)} all-reduce(f32[2,16,64]{2,1,0:T(8,128)S(1)} %reshape.56), channel_id=1, replica_groups=mesh['ctx'=8,'head'=4] {'ctx'}, use_global_device_ids=true, to_apply=%region_2.0 | all-reduce | flops 2048 | bytes 16384 | tf_op jit(solution)/shard_map/psum | solution.py:204
  143.5 0.1 reshape.53
  143.5 0.0 copy-done
  143.5 0.1 copy.25
  143.6 0.0 copy-done.2
  143.7 0.4 fusion.3
  144.0 0.1 copy.24
  144.1 0.1 copy.19
  144.2 0.1 copy.20
  144.3 0.1 copy.21
  144.4 0.0 copy-done.1
  144.5 0.0 copy-done.3
  144.5 0.7 copy.17.lists_ref
  145.2 38.6 %all-reduce.3.cloned.1.call-done = f32[2,16,64,128]{3,1,0,2:T(8,128)} async-done(((f32[2,16,64,128]{3,1,0,2:T(8,128)}), f32[2,16,64,128]{3,1,0,2:T(8,128)}) %all-reduce.3.cloned.1.call-update) | async-done | bytes 1048592 | tf_op jit(solution)/shard_map/psum | solution.py:204
  183.8 2.0 divide_convert_fusion
  185.8 8.8 %fusion = f32[64,2048]{1,0:T(8,128)S(1)} fusion(bf16[4096,2048]{1,0:T(8,128)(2,1)} %param.21, bf16[8,8,32,128]{3,2,1,0:T(8,128)(2,1)S(1)} %bitcast.28), kind=kOutput, calls=%fused_computation.4 | convolution fusion | flops 1073741824 | bytes 17825792 | tf_op jit(solution)/shard_map/dot_general | solution.py:215
  194.6 17.8 %all-reduce.4 = bf16[64,2048]{1,0:T(8,128)(2,1)} all-reduce(f32[64,2048]{1,0:T(8,128)S(1)} %fusion), channel_id=1, replica_groups=mesh['ctx'=8,'head'=4] {'head'}, use_global_device_ids=true, to_apply=%region_3.0 | all-reduce | flops 131072 | bytes 786432 | tf_op jit(solution)/shard_map/psum | solution.py:216
  212.4 13.4 %all-gather.3.cloned.1.call-done = bf16[2048,256]{1,0:T(8,128)(2,1)} async-done(((bf16[256,256]{1,0:T(8,128)(2,1)}), bf16[2048,256]{1,0:T(8,128)(2,1)}) %all-gather.3.cloned.1.call-update) | async-done | bytes 1048592 | tf_op jit(solution)/shard_map/all_gather | solution.py:175
  225.8 41.2 %all-gather.5.cloned.1.call-done = bf16[2048,256]{1,0:T(8,128)(2,1)} async-done(((bf16[256,256]{1,0:T(8,128)(2,1)}), bf16[2048,256]{1,0:T(8,128)(2,1)}) %all-gather.5.cloned.1.call-update) | async-done | bytes 1048592 | tf_op jit(solution)/shard_map/all_gather | solution.py:176
  267.0 34.6 %prefill.1 = (bf16[256,4096]{1,0:T(8,128)(2,1)}, bf16[1024,256]{1,0:T(8,128)(2,1)}, bf16[1024,256]{1,0:T(8,128)(2,1)}) custom-call(s32[16,6]{1,0:T(8,128)} %copy.17.lists_ref, s32[16]{0:T(128)} %owners_ref.1, bf16[256,4096]{1,0:T(8,128)(2,1)} %q_ref.2, bf16[16,128,256]{2,1,0:T(8,128)(2,1)} %bitcast.32, bf16[16,128,256]{2,1,0:T(8,128)(2,1)} %bitcast.33), custom_call_target="tpu_custom_call" | custom-call | flops 4294967296 | bytes 8388608 | tf_op jit(solution)/shard_map/prefill/pallas_call | solution.py:191
  (3 shorter events, 0.1 us)
Async XLA Ops:
  7.2 136.4 %copy-start = (bf16[64,4096]{1,0:T(8,128)(2,1)S(1)}, bf16[64,4096]{1,0:T(8,128)(2,1)}, u32[]{:S(2)}) copy-start(bf16[64,4096]{1,0:T(8,128)(2,1)} %q_ref.3) | copy-start | bytes 1572868
  7.2 136.5 %copy-start.2 = (bf16[64,256]{1,0:T(8,128)(2,1)S(1)}, bf16[64,256]{1,0:T(8,128)(2,1)}, u32[]{:S(2)}) copy-start(bf16[64,256]{1,0:T(8,128)(2,1)} %param.19) | copy-start | bytes 98308
  7.2 137.2 %copy-start.1 = (bf16[64,256]{1,0:T(8,128)(2,1)S(1)}, bf16[64,256]{1,0:T(8,128)(2,1)}, u32[]{:S(2)}) copy-start(bf16[64,256]{1,0:T(8,128)(2,1)} %param.20) | copy-start | bytes 98308
  7.2 137.3 %copy-start.3 = (s32[16,6]{0,1:T(8,128)S(1)}, s32[16,6]{0,1:T(8,128)}, u32[]{:S(2)}) copy-start(s32[16,6]{0,1:T(8,128)} %param.14) | copy-start | bytes 1156
  7.2 176.6 %all-reduce.3.cloned.1.call-start = ((), (), s32[]{:S(2)}) async-start(), calls=%async_computation.2 | async-start | bytes 2097152 | tf_op jit(solution)/shard_map/psum | solution.py:204
  106.4 119.4 %all-gather.3.cloned.1.call-start = ((), (), s32[]{:S(2)}) async-start(), calls=%async_computation | async-start | bytes 1179648 | tf_op jit(solution)/shard_map/all_gather | solution.py:175
  107.2 159.8 %all-gather.5.cloned.1.call-start = ((), (), s32[]{:S(2)}) async-start(), calls=%async_computation.1 | async-start | bytes 1179648 | tf_op jit(solution)/shard_map/all_gather | solution.py:176
Sparse Core Ops, SparseCore 0:
  106.5 77.1 all-reduce.2
  185.9 39.8 all-gather.2
  227.9 38.9 all-gather.4

commit v2 on v1

--- a/solution.py
+++ b/solution.py
@@ -37,7 +37,7 @@
 def decode_tile(dims, tile, q_ref, ck_ref, cv_ref, sk_ref, sv_ref, s_ref):
     samples, group, per, chunk = dims
     rows = per * samples
-    head = (tile * per) // group
+    head = lax.div(tile * per, group)
     q = jnp.concatenate([column(q_ref, tile * per + g, 0, samples) for g in range(per)], axis=0)
     resident = ck_ref.shape[0]
     high = jnp.full((rows, 128), NEG, jnp.float32)
@@ -141,86 +141,386 @@
             dst[rows, :] = jnp.where(live, x, 0.0).astype(jnp.bfloat16)
 
 
-def decode_kernel(dims, tiles, q_ref, ck_ref, cv_ref, sk_ref, sv_ref, m_ref, l_ref, acc_ref, s_ref):
-    samples, _, per, _ = dims
-
-    def step(tile, carry):
-        m, l, acc = decode_tile(dims, tile, q_ref, ck_ref, cv_ref, sk_ref, sv_ref, s_ref)
-        m_ref[tile] = jnp.broadcast_to(m, acc.shape)
-        l_ref[tile] = jnp.broadcast_to(l, acc.shape)
-        acc_ref[tile] = acc
+MESH = pl.DeviceIdType.MESH
+
+
+def pack_stats(m, l, rows):
+    lane = lax.broadcasted_iota(jnp.int32, (rows, 128), 1)
+    both = jnp.where(lane < 4, jnp.broadcast_to(m, (rows, 128)), jnp.broadcast_to(l, (rows, 128)))
+    if rows < 128:
+        both = jnp.concatenate([both] * (128 // rows), axis=0)
+    slabs = [both[i * 128 : (i + 1) * 128].T[:8] for i in range(max(1, rows // 128))]
+    return jnp.concatenate(slabs, axis=0)
+
+
+def unpack_stats(slabs, rows):
+    spread = [
+        jnp.concatenate([slabs[i * 8 : (i + 1) * 8]] * 16, axis=0).T for i in range(max(1, rows // 128))
+    ]
+    spread = jnp.concatenate(spread, axis=0)[:rows]
+    return spread[:, 0:1], spread[:, 4:5]
+
+
+def layer_kernel(
+    n_ctx,
+    n_head,
+    dims,
+    pre_dims,
+    lists_ref,
+    owners_ref,
+    q_ref,
+    sk_ref,
+    sv_ref,
+    sk_ref_own,
+    sv_ref_own,
+    span_k,
+    span_v,
+    ck_hbm,
+    cv_hbm,
+    sq_hbm,
+    w_hbm,
+    out_ref,
+    sample_ref,
+    ak_ref,
+    av_ref,
+    ck,
+    cv,
+    sq,
+    w,
+    kg,
+    vg,
+    s_ref,
+    kc,
+    vc,
+    part,
+    took,
+    att,
+    hpart,
+    htook,
+    hout,
+    in_sem,
+    g_send,
+    g_recv,
+    p_send,
+    p_recv,
+    a_send,
+    a_recv,
+    h_send,
+    h_recv,
+    o_send,
+    o_recv,
+):
+    samples, group, per, _ = dims
+    rows = per * samples
+    me = lax.axis_index("ctx")
+    hme = lax.axis_index("head")
+    qblk = span_k.shape[0]
+    n_hi = n_ctx // 2
+    hi, lo = lax.div(me, 2), lax.rem(me, 2)
+
+    def ctx(j):
+        return lax.rem(me + j + n_ctx, n_ctx)
+
+    def head(j):
+        return lax.rem(hme + j + n_head, n_head)
+
+    pair = hi * 2 + 1 - lo
+
+    local_copies = [
+        pltpu.make_async_copy(a, b, in_sem.at[i])
+        for i, (a, b) in enumerate(
+            (
+                (ck_hbm, ck),
+                (cv_hbm, cv),
+                (sq_hbm, sq),
+                (w_hbm, w),
+                (span_k, kg.at[pl.ds(me * qblk, qblk)]),
+                (span_v, vg.at[pl.ds(me * qblk, qblk)]),
+            )
+        )
+    ]
+    for i in (4, 5, 0, 1, 2, 3):
+        local_copies[i].start()
+    for i in (4, 5):
+        local_copies[i].wait()
+
+    barrier = pltpu.get_barrier_semaphore()
+    for j in range(1, n_ctx):
+        pl.semaphore_signal(barrier, inc=1, device_id={"ctx": ctx(j)}, device_id_type=MESH)
+    for j in range(1, n_head):
+        pl.semaphore_signal(barrier, inc=1, device_id={"head": head(j)}, device_id_type=MESH)
+    pl.semaphore_wait(barrier, n_ctx - 1 + n_head - 1)
+
+    def gather_copy(kind, index, src, owner, target):
+        full = (kg, vg)[kind]
+        view = full.at[pl.ds(owner * qblk, qblk)]
+        return pltpu.make_async_remote_copy(
+            src_ref=view if src is None else src,
+            dst_ref=view,
+            send_sem=g_send.at[kind, index],
+            recv_sem=g_recv.at[kind, index],
+            device_id={"ctx": target},
+            device_id_type=MESH,
+        )
+
+    for h in range(1, n_hi):
+        for kind, src in enumerate((span_k, span_v)):
+            gather_copy(kind, h, src, me, lax.rem(hi + h, n_hi) * 2 + lo).start()
+    for kind, src in enumerate((span_k, span_v)):
+        gather_copy(kind, 0, src, me, pair).start()
+
+    def forward(h):
+        owner = lax.rem(hi - h + n_hi, n_hi) * 2 + lo
+        for kind in range(2):
+            gather_copy(kind, h, None, owner, pair).wait_recv()
+        for kind in range(2):
+            gather_copy(kind, n_hi + h, None, owner, pair).start()
+
+    def part_copy(j):
+        return pltpu.make_async_remote_copy(
+            src_ref=part.at[j],
+            dst_ref=took.at[j],
+            send_sem=p_send.at[j],
+            recv_sem=p_recv.at[j],
+            device_id={"ctx": ctx(j)},
+            device_id_type=MESH,
+        )
+
+    for i in (0, 1):
+        local_copies[i].wait()
+
+    def one_tile(j):
+        m, l, acc = decode_tile(dims, ctx(j), q_ref, ck, cv, sk_ref, sv_ref, s_ref)
+        part[j, :rows, :] = acc
+        part[j, rows:, :] = pack_stats(m, l, rows)
+
+    def tile_step(j, carry):
+        one_tile(j)
+        part_copy(j).start()
         return carry
 
-    lax.fori_loop(0, tiles, step, 0)
-
-
-def prefill_kernel(dims, lists_ref, owners_ref, q_ref, kg_ref, vg_ref, out_ref, ak_ref, av_ref, kc_ref, vc_ref):
-    position = lax.axis_index("ctx")
-    append_all(position, owners_ref, kg_ref, vg_ref, ak_ref, av_ref)
-    prefill_all(dims, position, lists_ref, q_ref, kg_ref, vg_ref, kc_ref, vc_ref, out_ref)
+    points = min(3, n_hi - 1)
+    first, sent = 1, 1
+    for point in range(points):
+        last = n_ctx * (point + 2) // (points + 1)
+        lax.fori_loop(first, min(last, n_ctx), tile_step, 0)
+        first = min(last, n_ctx)
+        if point == points - 1:
+            lax.fori_loop(first, n_ctx, tile_step, 0)
+            one_tile(0)
+        until = 1 + (n_hi - 1) * (point + 1) // points
+        for h in range(sent, until):
+            forward(h)
+        sent = until
+
+    for i in (2,):
+        local_copies[i].wait()
+    for kind in range(2):
+        gather_copy(kind, 0, None, pair, pair).wait_recv()
+    for h in range(1, n_hi):
+        owner = lax.rem(hi - h + n_hi, n_hi) * 2 + 1 - lo
+        for kind in range(2):
+            gather_copy(kind, n_hi + h, None, owner, pair).wait_recv()
+
+    def att_copy(j):
+        return pltpu.make_async_remote_copy(
+            src_ref=att.at[0],
+            dst_ref=att.at[j],
+            send_sem=a_send.at[j],
+            recv_sem=a_recv.at[j],
+            device_id={"ctx": ctx(j)},
+            device_id_type=MESH,
+        )
+
+    def combine():
+        key_head = lax.div(me * per, group)
+        own_key = column(sk_ref_own, key_head, 0, samples).astype(jnp.float32)
+        own_value = column(sv_ref_own, key_head, 0, samples).astype(jnp.float32)
+        own = jnp.concatenate(
+            [
+                jnp.sum(
+                    column(q_ref, me * per + g, 0, samples).astype(jnp.float32) * own_key, axis=1, keepdims=True
+                )
+                for g in range(per)
+            ],
+            axis=0,
+        )
+        for j in range(1, n_ctx):
+            part_copy(j).wait_recv()
+        stats = [unpack_stats((took if j else part)[j, rows:, :], rows) for j in range(n_ctx)]
+        top = functools.reduce(jnp.maximum, [s[0] for s in stats] + [own])
+        new = jnp.exp2((own - top) * EXP2_SCALE)
+        total = new
+        acc = new * jnp.concatenate([own_value] * per, axis=0)
+        for j in range(n_ctx):
+            factor = jnp.exp2((stats[j][0] - top) * EXP2_SCALE)
+            total = total + factor * stats[j][1]
+            acc = acc + factor * (took if j else part)[j, :rows, :]
+        attended = (acc / total).astype(jnp.bfloat16)
+        for g in range(per):
+            att[0, :, g * HD : (g + 1) * HD] = attended[g * samples : (g + 1) * samples]
+        for j in range(1, n_ctx):
+            att_copy(j).start()
+
+    columns = w.shape[1] // n_head
+    depth = per * HD
+
+    def head_copy(j):
+        return pltpu.make_async_remote_copy(
+            src_ref=hpart.at[j],
+            dst_ref=htook.at[j],
+            send_sem=h_send.at[j],
+            recv_sem=h_recv.at[j],
+            device_id={"head": head(j)},
+            device_id_type=MESH,
+        )
+
+    def project():
+        for j in range(1, n_ctx):
+            att_copy(j).wait_recv()
+        local_copies[3].wait()
+        for j in [*range(1, n_head), 0]:
+            where = pl.ds(pl.multiple_of(head(j) * columns, 128), columns)
+            total = jnp.zeros((samples, columns), jnp.float32)
+            for c in range(n_ctx):
+                total = total + dot(att[c], w[pl.ds(pl.multiple_of(ctx(-c) * depth, 128), depth), where])
+            hpart[j] = total
+            if j:
+                head_copy(j).start()
+
+    def out_copy(j):
+        return pltpu.make_async_remote_copy(
+            src_ref=hout.at[0],
+            dst_ref=hout.at[j],
+            send_sem=o_send.at[j],
+            recv_sem=o_recv.at[j],
+            device_id={"head": head(j)},
+            device_id_type=MESH,
+        )
+
+    def between(unit):
+        if unit == COMBINE_AFTER:
+            combine()
+        if unit == PROJECT_AFTER:
+            project()
+
+    prefill_all(pre_dims, me, lists_ref, sq, kg, vg, kc, vc, out_ref, between)
+    for j in range(1, n_head):
+        head_copy(j).wait_recv()
+    total = hpart[0]
+    for j in range(1, n_head):
+        total = total + htook[j]
+    hout[0] = total.astype(jnp.bfloat16)
+    for j in range(1, n_head):
+        out_copy(j).start()
+    append_all(me, owners_ref, kg, vg, ak_ref, av_ref)
+    for j in range(1, n_head):
+        out_copy(j).wait_recv()
+    for j in range(n_head):
+        sample_ref[:, pl.ds(pl.multiple_of(head(-j) * columns, 128), columns)] = hout[j]
+
+    for kind, src in enumerate((span_k, span_v)):
+        for h in range(n_hi):
+            gather_copy(kind, h, src, me, pair).wait_send()
+        for h in range(1, n_hi):
+            gather_copy(kind, n_hi + h, None, me, pair).wait_send()
+    for j in range(1, n_ctx):
+        part_copy(j).wait_send()
+        att_copy(j).wait_send()
+    for j in range(1, n_head):
+        head_copy(j).wait_send()
+        out_copy(j).wait_send()
 
 
 VM = pl.BlockSpec(memory_space=pltpu.VMEM)
 SM = pl.BlockSpec(memory_space=pltpu.SMEM)
-
-
-def local(n_ctx, span_query, span_key, span_value, block_lists, owners, cache_key, cache_value, sample_query, sample_key, sample_value, out_weight):
+ANY = pl.BlockSpec(memory_space=pl.ANY)
+COMBINE_AFTER = 1
+PROJECT_AFTER = 3
+
+
+def local(n_ctx, n_head, span_query, span_key, span_value, block_lists, owners, cache_key, cache_value, sample_query, sample_key, sample_value, out_weight):
     tokens = span_query.shape[0]
     kvh = span_key.shape[1] // HD
     group = span_query.shape[1] // HD // kvh
     qblk = tokens // BLOCK
     samples = sample_query.shape[0]
     per = kvh * group // n_ctx
+    rows = per * samples
     resident = cache_key.shape[0]
-    kg = lax.all_gather(span_key, "ctx", axis=0, tiled=True).reshape(-1, BLOCK, kvh * HD)
-    vg = lax.all_gather(span_value, "ctx", axis=0, tiled=True).reshape(-1, BLOCK, kvh * HD)
-    dims = (samples, group, per, 512)
-    f32 = jax.ShapeDtypeStruct((n_ctx, per * samples, HD), jnp.float32)
-    m, l, acc = pl.pallas_call(
-        functools.partial(decode_kernel, dims, n_ctx),
-        out_shape=(f32, f32, f32),
-        in_specs=[VM] * 5,
-        out_specs=(VM,) * 3,
-        scratch_shapes=[pltpu.VMEM((per * samples, resident), jnp.float32)],
-        compiler_params=pltpu.CompilerParams(vmem_limit_bytes=60 << 20),
-        cost_estimate=pl.CostEstimate(flops=5 << 30, bytes_accessed=8 << 20, transcendentals=9 << 20),
-        name="decode",
-    )(sample_query, cache_key, cache_value, span_key, span_value)
-    width = (block_lists.shape[1] + 1) * BLOCK
-    slots = jax.ShapeDtypeStruct((MOST_BLOCKS * BLOCK, kvh * HD), jnp.bfloat16)
-    span_out, appended_key, appended_value = pl.pallas_call(
-        functools.partial(prefill_kernel, (qblk, kvh, group, block_lists.shape[1], 4)),
-        out_shape=(jax.ShapeDtypeStruct(span_query.shape, jnp.bfloat16), slots, slots),
-        in_specs=[SM, SM, VM, VM, VM],
-        out_specs=(VM,) * 3,
-        scratch_shapes=[pltpu.VMEM((width, kvh * HD), jnp.bfloat16)] * 2,
-        compiler_params=pltpu.CompilerParams(vmem_limit_bytes=60 << 20),
-        cost_estimate=pl.CostEstimate(flops=4 << 30, bytes_accessed=8 << 20, transcendentals=7 << 20),
-        name="prefill",
-    )(block_lists, owners, span_query, kg, vg)
-    m, l = m[:, :, :1] * SCALE, l[:, :, :1]
-    top = lax.pmax(m, "ctx")
-    factor = jnp.exp(m - top)
-    l, acc = lax.psum((l * factor, acc * factor), "ctx")
-    shape = (kvh, group, samples, -1)
-    top, l, acc = top.reshape(shape), l.reshape(shape), acc.reshape(shape)
-    asked = sample_query.reshape(samples, kvh, group, HD)
-    own_keys = sample_key.reshape(samples, kvh, HD)
-    own = jnp.einsum("skgd,skd->kgs", asked, own_keys, preferred_element_type=jnp.float32)[..., None] * SCALE
-    own_values = jnp.transpose(sample_value.reshape(samples, kvh, HD).astype(jnp.float32), (1, 0, 2))[:, None]
-    final = jnp.maximum(top, own)
-    old, new = jnp.exp(top - final), jnp.exp(own - final)
-    attended = ((acc * old + new * own_values) / (l * old + new)).astype(jnp.bfloat16)
-    attended = jnp.transpose(attended, (2, 0, 1, 3)).reshape(samples, -1)
-    partial_out = jnp.dot(attended, out_weight, preferred_element_type=jnp.float32)
-    sample_out = lax.psum(partial_out, "head").astype(jnp.bfloat16)
-    return span_out, sample_out, appended_key, appended_value
+    ksel = block_lists.shape[1]
+    width = (ksel + 1) * BLOCK
+    wide = kvh * HD
+    columns = out_weight.shape[1] // n_head
+    packet = rows + 8 * max(1, rows // 128)
+    bf16, f32 = jnp.bfloat16, jnp.float32
+    slots = jax.ShapeDtypeStruct((MOST_BLOCKS * BLOCK, wide), bf16)
+    dma = pltpu.SemaphoreType.DMA
+    return pl.pallas_call(
+        functools.partial(
+            layer_kernel, n_ctx, n_head, (samples, group, per, 512), (qblk, kvh, group, ksel, 4)
+        ),
+        out_shape=(
+            jax.ShapeDtypeStruct(span_query.shape, bf16),
+            jax.ShapeDtypeStruct((samples, out_weight.shape[1]), bf16),
+            slots,
+            slots,
+        ),
+        in_specs=[SM, SM] + [VM] * 5 + [ANY] * 6,
+        out_specs=(VM,) * 4,
+        scratch_shapes=[
+            pltpu.VMEM(cache_key.shape, bf16),
+            pltpu.VMEM(cache_value.shape, bf16),
+            pltpu.VMEM(span_query.shape, bf16),
+            pltpu.VMEM(out_weight.shape, bf16),
+            pltpu.VMEM((block_lists.shape[0], BLOCK, wide), bf16),
+            pltpu.VMEM((block_lists.shape[0], BLOCK, wide), bf16),
+            pltpu.VMEM((rows, resident), f32),
+            pltpu.VMEM((width, wide), bf16),
+            pltpu.VMEM((width, wide), bf16),
+            pltpu.VMEM((n_ctx, packet, HD), f32),
+            pltpu.VMEM((n_ctx, packet, HD), f32),
+            pltpu.VMEM((n_ctx, samples, per * HD), bf16),
+            pltpu.VMEM((n_head, samples, columns), f32),
+            pltpu.VMEM((n_head, samples, columns), f32),
+            pltpu.VMEM((n_head, samples, columns), bf16),
+            dma((6,)),
+            dma((2, n_ctx)),
+            dma((2, n_ctx)),
+            dma((n_ctx,)),
+            dma((n_ctx,)),
+            dma((n_ctx,)),
+            dma((n_ctx,)),
+            dma((n_head,)),
+            dma((n_head,)),
+            dma((n_head,)),
+            dma((n_head,)),
+        ],
+        compiler_params=pltpu.CompilerParams(
+            vmem_limit_bytes=62 << 20, collective_id=0, has_side_effects=True
+        ),
+        name="layer",
+    )(
+        block_lists,
+        owners,
+        sample_query,
+        span_key,
+        span_value,
+        sample_key,
+        sample_value,
+        span_key.reshape(qblk, BLOCK, wide),
+        span_value.reshape(qblk, BLOCK, wide),
+        cache_key,
+        cache_value,
+        span_query,
+        out_weight,
+    )
 
 
 def solution(mesh):
     c = P("ctx", "head")
     return jax.shard_map(
-        functools.partial(local, mesh.shape["ctx"]),
+        functools.partial(local, mesh.shape["ctx"], mesh.shape["head"]),
         mesh=mesh,
         in_specs=(c, c, c, P(), P(), c, c, P(None, "head"), P(None, "head"), P(None, "head"), P("head", "ctx")),
         out_specs=(c, P(None, "ctx"), c, c),

time: 308 us -> 105 us (0.34)
  blocking collectives: 127 us -> 0 us
  waiting for transfers between devices: 94.6 us -> 0 us
  Pallas kernels: 53 us -> 95.5 us
  between operations: 13.9 us -> 0.67 us
  matrix products: 9.19 us -> 0 us
  other arithmetic: 7.35 us -> 0 us
  local copies, waits for them, and re-layouts: 2.91 us -> 6.89 us
    pmax x1 -> x0, blocking collectives: 73.8 us -> none  [local(): top = lax.pmax(m, 'ctx')]
    all_gather x2 -> x0, waiting for transfers between devices: 54.6 us -> none  [the longest x1 41.2 us: local(): lax.all_gather(span_value, 'ctx', axis=0, tiled=True)]
    psum x2 -> x0, blocking collectives: 53.2 us -> none  [the longest x1 35.5 us: local(): l, acc = lax.psum((l * factor, acc * factor), 'ctx')]
    pallas_call x2 -> x1, Pallas kernels: 53 us -> 95.5 us  [local(): pl.pallas_call(functools.partial(layer_kernel, n_ctx, n_head, (samples, g...]
    psum x1 -> x0, waiting for transfers between devices: 38.6 us -> none  [local(): l, acc = lax.psum((l * factor, acc * factor), 'ctx')]
    dot_general x2 -> x0, matrix products: 9.19 us -> none  [the longest x1 8.81 us: local(): jnp.dot(attended, out_weight, preferred_element_type=jnp.float32)]
    unnamed x10 -> x11, local copies, waits for them, and re-layouts: 0.79 us -> 6.89 us
    mul x3 -> x0, other arithmetic: 5.32 us -> none  [the longest x2 4 us: local(): l, acc = lax.psum((l * factor, acc * factor), 'ctx')]
  transfers between devices with their start and end apart: 3 -> 0, of which waited for: 3 -> 0; matrix products, arithmetic and copies ran while one was open for 4% -> 0% of each run, Pallas kernels for 0% -> 0%
where the time goes in v2:
time: 105 us; the launch traced here: 103 us
  Pallas kernels  95.5 us (91%)
  local copies, waits for them, and re-layouts  6.89 us (7%)
    pallas_call x1, Pallas kernels, local(): pl.pallas_call(functools.partial(layer_kernel, n_ctx, n_head, (samples, g...  95.5 us
    unnamed x11, local copies, waits for them, and re-layouts  6.89 us

profile of v2, /device:TPU:0, one launch (start us, length us, event | category | flops | bytes accessed | tf_op | source)
XLA Modules:
  0.0 103.1 jit_solution(2478250865649941233)
XLA Ops:
  0.6 1.4 %copy.15.lists_ref = s32[16,6]{1,0:T(8,128)} copy(s32[16,6]{0,1:T(8,128)} %param.14) | data formatting | bytes 768 | tf_op args[3]
  2.0 95.5 %layer.1 = (bf16[256,4096]{1,0:T(8,128)(2,1)}, bf16[64,2048]{1,0:T(8,128)(2,1)}, bf16[1024,256]{1,0:T(8,128)(2,1)}, bf16[1024,256]{1,0:T(8,128)(2,1)}) custom-call(s32[16,6]{1,0:T(8,128)} %copy.15.lists_ref, s32[16]{0:T(128)} %owners_ref.1, bf16[64,4096]{1,0:T(8,128)(2,1)} %q_ref.1, bf16[256,256]{1,0:T(8,128)(2,1)} %sk_ref.1, bf16[256,256]{1,0:T(8,128)(2,1)} %sv_ref.1, ...), custom_call_target="tpu_custom_call" | custom-call | tf_op jit(solution)/shard_map/layer/pallas_call | solution.py:459
  97.5 0.0 copy-start.2
  97.5 0.0 copy-start.1
  97.6 0.0 copy-start
  97.6 3.2 %copy.20 = bf16[256,4096]{1,0:T(8,128)(2,1)} copy(bf16[256,4096]{1,0:T(8,128)(2,1)} %get-tuple-element.8) | data formatting | bytes 4194304
  100.8 0.0 copy-done.2
  100.8 0.7 copy.21
  101.5 0.0 copy-done.1
  101.5 0.8 copy.22
  102.3 0.0 copy-done
  102.3 0.8 copy.23
Async XLA Ops:
  97.5 3.3 %copy-start.2 = (bf16[64,2048]{1,0:T(8,128)(2,1)S(1)}, bf16[64,2048]{1,0:T(8,128)(2,1)}, u32[]{:S(2)}) copy-start(bf16[64,2048]{1,0:T(8,128)(2,1)} %get-tuple-element.9) | copy-start | bytes 786436
  97.5 4.0 %copy-start.1 = (bf16[1024,256]{1,0:T(8,128)(2,1)S(1)}, bf16[1024,256]{1,0:T(8,128)(2,1)}, u32[]{:S(2)}) copy-start(bf16[1024,256]{1,0:T(8,128)(2,1)} %get-tuple-element.10) | copy-start | bytes 1572868
  97.6 4.7 %copy-start = (bf16[1024,256]{1,0:T(8,128)(2,1)S(1)}, bf16[1024,256]{1,0:T(8,128)(2,1)}, u32[]{:S(2)}) copy-start(bf16[1024,256]{1,0:T(8,128)(2,1)} %get-tuple-element.11) | copy-start | bytes 1572868
